TPU v7x, 512 devices: a whole 4x8x8 slice. The times are simulated.
512 devices in a mesh: tm: 32 (over x, z), space: 16 (over y, core).
Axes of the slice: x: 4, y: 8, z: 8, core: 2. Of those that a mesh axis runs over, the one named last changes fastest.
Arguments:
- inverse_factor: bfloat16 [32, 2048, 2048], P('tm', None, 'space'), as said below
- arrow_factor: bfloat16 [32, 64, 2048], P('tm', None, 'space'), may hold values from -6 to 6
- decay: float32 [32, 2048], P('tm'), may hold values from 0 to 1
- tip_inverse: float32 [64, 64], replicated, may hold values from -0.75 to 0.75
- sigma_end: float32 [2048, 2048], P(None, 'space'), may hold values from -2.7 to 2.7, as said below
- arrow_end: float32 [2048, 64], P('space'), may hold values from -6 to 6
Outputs:
- sigmas: float32 [32, 2048, 2048], P('tm', None, 'space')
- arrows: float32 [32, 2048, 64], P('tm', 'space')
Inputs may be any that keep to these rules, and one draw needn't show every extreme that they name: `inverse_factor`: each K_t is lower triangular with a positive diagonal. `sigma_end`: symmetric.
All inputs are finite; a program needn't handle non-finite values.
Results may differ from a plain program's by a relative error of at most 0.0003.
Values may be sent and summed in bfloat16 or wider, within the bound.
No kernel may reach another device: no remote copies, remote signals or barrier semaphores. Data moves between devices by JAX's collectives and lax.ppermute only.
A program may use at most 128 MiB of HBM per device.

v0:
```python
import jax
import jax.numpy as jnp
from jax import lax
from jax.sharding import PartitionSpec as P


def prefix(array, axis, combine, identity):
    devices, position = (lax.axis_size(axis), lax.axis_index(axis))
    everything = jax.tree.map(lambda part: lax.all_gather(part, axis), array)
    start = jax.tree.map(
        lambda part, zero: jnp.broadcast_to(jnp.asarray(zero, part.dtype), part.shape),
        array,
        identity,
    )

    def hop(k, before):
        at = devices - 1 - k
        reached = at > position
        new = combine(before, jax.tree.map(lambda part: part[at], everything))
        return jax.tree.map(lambda a, b: jnp.where(reached, a, b), new, before)

    return lax.fori_loop(0, devices, hop, start)


def column_products(left, right):
    return lax.dot_general(
        left, right, (((0,), (0,)), ((), ())), preferred_element_type=jnp.float32
    )


def compose(earlier, later):
    falloff_later, own_after, sigma_after, arrow_after = earlier
    lower_factor_current, own_here, sigma_here, border_column_current = later
    return (
        lower_factor_current * falloff_later,
        own_here * own_after,
        sigma_here + lower_factor_current[:, None] * own_here[None, :] * sigma_after,
        border_column_current + own_here[:, None] * arrow_after,
    )


def body(inverse_factor, arrow_factor, decay, tip_inverse, sigma_end, arrow_end):
    highest = lax.Precision.HIGHEST
    factor_cols = inverse_factor[0]
    order = factor_cols.shape[0]
    width = factor_cols.shape[1]
    panel_index = lax.axis_index("space")
    precision_panel = column_products(
        lax.all_gather(factor_cols, "space", axis=1, tiled=True), factor_cols
    )
    decay_all = decay[0]
    self_falloff = lax.dynamic_slice_in_dim(decay_all, panel_index * width, width)
    arrow_local = arrow_factor[0]
    arrow_wide = arrow_local.astype(jnp.float32)
    cross = lax.psum_scatter(
        lax.dot_general(
            precision_panel,
            arrow_wide,
            (((1,), (1,)), ((), ())),
            precision=highest,
            preferred_element_type=jnp.float32,
        ),
        "space",
        scatter_dimension=0,
        tiled=True,
    )
    own_arrow = -jnp.dot(cross, tip_inverse, precision=highest)
    arrow_cols_count = tip_inverse.shape[0]
    identity_matrix = (
        jnp.ones((order,), jnp.float32),
        jnp.ones((width,), jnp.float32),
        jnp.zeros((order, width), jnp.float32),
        jnp.zeros((width, arrow_cols_count), jnp.float32),
    )
    mine = (decay_all, self_falloff, precision_panel, own_arrow)
    later_decay, later_own, later_sigma, later_arrow = prefix(mine, "tm", compose, identity_matrix)
    covariance_following = later_sigma + later_decay[:, None] * later_own[None, :] * sigma_end
    spike_ahead = later_arrow + later_own[:, None] * arrow_end
    sigma_block = (
        precision_panel + decay_all[:, None] * self_falloff[None, :] * covariance_following
    )
    arrow_block = own_arrow + self_falloff[:, None] * spike_ahead
    return (sigma_block[None], arrow_block[None])


def solution(mesh):
    placed = (
        P("tm", None, "space"),
        P("tm", None, "space"),
        P("tm", None),
        P(),
        P(None, "space"),
        P("space", None),
    )
    return jax.shard_map(
        body,
        mesh=mesh,
        in_specs=placed,
        out_specs=(P("tm", None, "space"), P("tm", "space", None)),
        check_vma=False,
    )
```

profile of v0, /device:TPU:1, one launch (start us, length us, event | category | flops | bytes accessed | tf_op | source)
XLA Modules:
  0.0 611.4 jit_solution(3542080441122480926)
XLA Ops:
  8.0 76.7 %all-gather.9.cloned.1.call-done = bf16[1,2048,2048]{2,1,0:T(8,128)(2,1)} async-done(((bf16[1,2048,128]{2,1,0:T(8,128)(2,1)}), bf16[1,2048,2048]{2,1,0:T(8,128)(2,1)}) %all-gather.9.cloned.1.call-update) | async-done | bytes 8388624 | tf_op jit(solution)/shard_map/all_gather | solution.py:49
  84.7 5.8 fusion.3
  92.2 54.2 %reduce-scatter.2.cloned.1.call-done = f32[128,64]{1,0:T(8,128)} async-done(((f32[2048,64]{1,0:T(8,128)}), f32[128,64]{1,0:T(8,128)}) %reduce-scatter.2.cloned.1.call-update) | async-done | bytes 32784 | tf_op jit(solution)/shard_map/reduce_scatter | solution.py:55
  148.8 37.9 %all-gather.3 = f32[32,1,2048]{2,1,0:T(1,128)S(1)} all-gather(f32[1,1,2048]{2,1,0:T(1,128)S(1)} %bitcast.51), channel_id=1, replica_groups=mesh['tm'=32,'space'=16] {'tm'}, dimensions={0}, use_global_device_ids=true | all-gather | bytes 270336 | tf_op jit(solution)/shard_map/all_gather | solution.py:9
  187.4 33.0 %all-gather.4 = f32[32,1,128]{2,1,0:T(1,128)} all-gather(f32[1,1,128]{2,1,0:T(1,128)S(1)} %get-tuple-element.327), channel_id=1, replica_groups=mesh['tm'=32,'space'=16] {'tm'}, dimensions={0}, use_global_device_ids=true | all-gather | bytes 16896 | tf_op jit(solution)/shard_map/all_gather | solution.py:9
  220.4 4.0 all-gather.13.cloned.1.call-done
  224.4 3.1 copy.12
  227.5 243.0 %all-gather.11.cloned.1.call-done = f32[65536,128]{1,0:T(8,128)} async-done(((f32[2048,128]{1,0:T(8,128)}), f32[65536,128]{1,0:T(8,128)}) %all-gather.11.cloned.1.call-update) | async-done | bytes 33554448 | tf_op jit(solution)/shard_map/all_gather | solution.py:9
  470.5 130.7 %while.22 = (s32[]{:T(128)}, f32[2048]{0:T(1024)S(1)}, f32[128]{0:T(128)}, f32[2048,128]{1,0:T(8,128)S(1)}, f32[128,64]{1,0:T(8,128)S(1)}, /*index=5*/s32[]{:T(1...) while((s32[]{:T(128)}, f32[2048]{0:T(1024)S(1)}, ...), condition=%wide.region_2.3_spmd.clone, body=%wide.region_1.2_spmd.clone.sunk | while | flops 1350024 | bytes 3296485 | solution.py:22
  472.9 1.8 fusion.16
  477.0 1.8 fusion.16
  481.1 1.8 fusion.16
  485.2 1.8 fusion.16
  489.3 1.8 fusion.16
  493.3 1.8 fusion.16
  497.4 1.8 fusion.16
  501.5 1.8 fusion.16
  505.6 1.8 fusion.16
  509.7 1.8 fusion.16
  513.8 1.8 fusion.16
  517.8 1.8 fusion.16
  521.9 1.8 fusion.16
  526.0 1.8 fusion.16
  530.1 1.8 fusion.16
  534.2 1.8 fusion.16
  538.2 1.8 fusion.16
  542.3 1.8 fusion.16
  546.4 1.8 fusion.16
  550.5 1.8 fusion.16
  554.5 1.8 fusion.16
  558.6 1.8 fusion.16
  602.7 2.2 add_bitcast_fusion
  (170 shorter events, 96.7 us)
Async XLA Ops:
  7.2 139.2 %copy-start = (f32[64,64]{1,0:T(8,128)S(1)}, f32[64,64]{1,0:T(8,128)}, u32[]{:S(2)}) copy-start(f32[64,64]{1,0:T(8,128)} %param.11) | copy-start | bytes 49156
  7.2 83.3 %copy-start.6 = (bf16[1,64,128]{2,1,0:T(8,128)(2,1)S(1)}, bf16[1,64,128]{2,1,0:T(8,128)(2,1)}, u32[]{:S(2)}) copy-start(bf16[1,64,128]{2,1,0:T(8,128)(2,1)} %param.9) | copy-start | bytes 49156
  7.2 77.5 %all-gather.9.cloned.1.call-start = ((), (), s32[]{:S(2)}) async-start(), calls=%async_computation.2 | async-start | bytes 8912896 | tf_op jit(solution)/shard_map/all_gather | solution.py:49
  7.9 140.9 %copy-start.5 = (f32[1,2048]{1,0:T(1,128)S(1)}, f32[1,2048]{1,0:T(1,128)}, u32[]{:S(2)}) copy-start(f32[1,2048]{1,0:T(1,128)} %param.10) | copy-start | bytes 24580
  7.9 138.5 %reduce-scatter.2.cloned.1.call-start = ((), (), s32[]{:S(2)}) async-start(), calls=%async_computation.1 | async-start | bytes 1114112 | tf_op jit(solution)/shard_map/reduce_scatter | solution.py:55
  90.5 57.7 %copy-start.1 = (f32[2048,128]{1,0:T(8,128)}, f32[2048,128]{1,0:T(8,128)S(1)}, u32[]{:S(2)}) copy-start(f32[2048,128]{1,0:T(8,128)S(1)} %fusion.3) | copy-start | bytes 3145732
  92.1 132.3 %all-gather.13.cloned.1.call-start = ((), (), s32[]{:S(2)}) async-start(), calls=%async_computation.4 | async-start | bytes 1081344 | tf_op jit(solution)/shard_map/all_gather | solution.py:9
  148.1 322.3 %all-gather.11.cloned.1.call-start = ((), (), s32[]{:S(2)}) async-start(), calls=%async_computation.3 | async-start | bytes 34603008 | tf_op jit(solution)/shard_map/all_gather | solution.py:9
  470.5 130.8 %copy-start.4 = (f32[128,64]{0,1:T(8,128)S(1)}, f32[128,64]{0,1:T(8,128)}, u32[]{:S(2)}) copy-start(f32[128,64]{0,1:T(8,128)} %convolution_negate_fusion) | copy-start | bytes 98308
  470.5 132.2 %copy-start.2 = (f32[2048,128]{1,0:T(8,128)S(1)}, f32[2048,128]{1,0:T(8,128)}, u32[]{:S(2)}) copy-start(f32[2048,128]{1,0:T(8,128)} %copy-done.1) | copy-start | bytes 3145732
  470.5 132.2 %copy-start.3 = (f32[2048,128]{1,0:T(8,128)S(1)}, f32[2048,128]{1,0:T(8,128)}, u32[]{:S(2)}) copy-start(f32[2048,128]{1,0:T(8,128)} %param.12) | copy-start | bytes 3145732
Sparse Core Ops, SparseCore 0:
  10.1 74.5 all-gather.8
  92.2 54.1 reduce-scatter.1
  150.5 73.8 all-gather.12
  228.5 241.9 all-gather.10
where the time goes:
time: 615 us; the launch traced here: 611 us
  waiting for transfers between devices  379 us (62%)
  other arithmetic  132 us (21%)
  blocking collectives  70.9 us (12%)
  between operations  13.9 us (2%)
  matrix products  9.12 us (1%)
    all_gather x2, waiting for transfers between devices, prefix(): everything = jax.tree.map(lambda part: lax.all_gather(part, axis), array)  247 us
    select_n x128, other arithmetic, hop(): return jax.tree.map(lambda a, b: jnp.where(reached, a, b), new, before)  129 us
    all_gather x1, waiting for transfers between devices, body(): lax.all_gather(factor_cols, 'space', axis=1, tiled=True)  76.7 us
    all_gather x2, blocking collectives, prefix(): everything = jax.tree.map(lambda part: lax.all_gather(part, axis), array)  70.9 us
    reduce_scatter x1, waiting for transfers between devices, body(): lax.psum_scatter(lax.dot_general(precision_panel, arrow_wide, (((1,), (1,...  54.2 us
  transfers between devices with their start and end apart: 4, of which 4 were waited for; matrix products, arithmetic and copies ran while one was open for 1% of the time, Pallas kernels for 0%

commit v1 on v0

--- a/solution.py
+++ b/solution.py
@@ -2,6 +2,13 @@
 import jax.numpy as jnp
 from jax import lax
 from jax.sharding import PartitionSpec as P
+
+drive_orders = lambda raw: jnp.concatenate(
+    lax.all_to_all(
+        jnp.stack(lax.axis_size("space") * [raw]), axis_name="space", split_axis=0, concat_axis=0
+    ),
+    axis=1,
+)
 
 
 def prefix(array, axis, combine, identity):
@@ -45,9 +52,7 @@
     order = factor_cols.shape[0]
     width = factor_cols.shape[1]
     panel_index = lax.axis_index("space")
-    precision_panel = column_products(
-        lax.all_gather(factor_cols, "space", axis=1, tiled=True), factor_cols
-    )
+    precision_panel = column_products(drive_orders(factor_cols), factor_cols)
     decay_all = decay[0]
     self_falloff = lax.dynamic_slice_in_dim(decay_all, panel_index * width, width)
     arrow_local = arrow_factor[0]

time: 615 us -> 734 us (1.19)
  blocking collectives: 70.9 us -> 266 us
  waiting for transfers between devices: 379 us -> 304 us
    all_to_all x0 -> x1, blocking collectives: none -> 195 us  [lax.all_to_all(jnp.stack(lax.axis_size('space') * [raw]), axis_name='spac...]
    all_gather x1 -> x0, waiting for transfers between devices: 76.7 us -> none  [body(): lax.all_gather(factor_cols, 'space', axis=1, tiled=True)]
  transfers between devices with their start and end apart: 4 -> 3, of which waited for: 4 -> 3; matrix products, arithmetic and copies ran while one was open for 1% -> 1% of each run, Pallas kernels for 0% -> 0%
where the time goes in v1:
time: 734 us; the launch traced here: 730 us
  waiting for transfers between devices  304 us (41%)
  blocking collectives  266 us (36%)
  other arithmetic  132 us (18%)
  between operations  13.9 us (2%)
    all_gather x2, waiting for transfers between devices, prefix(): everything = jax.tree.map(lambda part: lax.all_gather(part, axis), array)  247 us
    all_to_all x1, blocking collectives, lax.all_to_all(jnp.stack(lax.axis_size('space') * [raw]), axis_name='spac...  195 us
    select_n x128, other arithmetic, hop(): return jax.tree.map(lambda a, b: jnp.where(reached, a, b), new, before)  128 us
    all_gather x2, blocking collectives, prefix(): everything = jax.tree.map(lambda part: lax.all_gather(part, axis), array)  70.9 us
    reduce_scatter x1, waiting for transfers between devices, body(): lax.psum_scatter(lax.dot_general(precision_panel, arrow_wide, (((1,), (1,...  56 us
  transfers between devices with their start and end apart: 3, of which 3 were waited for; matrix products, arithmetic and copies ran while one was open for 1% of the time, Pallas kernels for 0%

profile of v1, /device:TPU:1, one launch (start us, length us, event | category | flops | bytes accessed | tf_op | source)
XLA Modules:
  0.0 729.7 jit_solution(772179466245330066)
XLA Ops:
  9.6 195.4 %all_to_all.5 = bf16[16,2048,128]{1,2,0:T(8,128)(2,1)S(1)} all-to-all(bf16[16,2048,128]{1,2,0:T(8,128)(2,1)S(1)} %stack.3), channel_id=1, replica_groups=mesh['tm'=32,'space'=16] {'space'}, dimensions={0} | all-to-all | bytes 16777216 | tf_op jit(solution)/shard_map/all_to_all | solution.py:7
  205.0 2.4 fusion.7
  209.0 56.0 %reduce-scatter.2.cloned.1.call-done = f32[128,64]{0,1:T(8,128)} async-done(((f32[2048,64]{0,1:T(8,128)}), f32[128,64]{0,1:T(8,128)}) %reduce-scatter.2.cloned.1.call-update) | async-done | bytes 32784 | tf_op jit(solution)/shard_map/reduce_scatter | solution.py:60
  267.4 37.8 %all-gather.2 = f32[32,1,2048]{2,1,0:T(1,128)S(1)} all-gather(f32[1,1,2048]{2,1,0:T(1,128)S(1)} %bitcast.54), channel_id=1, replica_groups=mesh['tm'=32,'space'=16] {'tm'}, dimensions={0}, use_global_device_ids=true | all-gather | bytes 270336 | tf_op jit(solution)/shard_map/all_gather | solution.py:16
  306.0 33.1 %all-gather.3 = f32[32,1,128]{2,1,0:T(1,128)} all-gather(f32[1,1,128]{2,1,0:T(1,128)S(1)} %get-tuple-element.337), channel_id=1, replica_groups=mesh['tm'=32,'space'=16] {'tm'}, dimensions={0}, use_global_device_ids=true | all-gather | bytes 16896 | tf_op jit(solution)/shard_map/all_gather | solution.py:16
  339.0 4.0 all-gather.9.cloned.1.call-done
  343.0 3.1 copy.16
  346.2 243.1 %all-gather.7.cloned.1.call-done = f32[65536,128]{1,0:T(8,128)} async-done(((f32[2048,128]{1,0:T(8,128)}), f32[65536,128]{1,0:T(8,128)}) %all-gather.7.cloned.1.call-update) | async-done | bytes 33554448 | tf_op jit(solution)/shard_map/all_gather | solution.py:16
  589.3 130.2 %while.22 = (s32[]{:T(128)}, f32[2048]{0:T(1024)S(1)}, f32[128]{0:T(128)}, f32[2048,128]{1,0:T(8,128)S(1)}, f32[128,64]{1,0:T(8,128)S(1)}, /*index=5*/s32[]{:T(1...) while((s32[]{:T(128)}, f32[2048]{0:T(1024)S(1)}, ...), condition=%wide.region_2.3_spmd.clone, body=%wide.region_1.2_spmd.clone.sunk | while | flops 1350024 | bytes 3296485 | solution.py:29
  591.7 1.8 fusion.16
  595.7 1.8 fusion.16
  599.8 1.8 fusion.16
  603.8 1.8 fusion.16
  607.9 1.8 fusion.16
  612.0 1.8 fusion.16
  616.0 1.8 fusion.16
  620.1 1.8 fusion.16
  624.1 1.8 fusion.16
  628.2 1.8 fusion.16
  632.3 1.8 fusion.16
  636.3 1.8 fusion.16
  640.4 1.8 fusion.16
  644.4 1.8 fusion.16
  648.5 1.8 fusion.16
  652.6 1.8 fusion.16
  656.6 1.8 fusion.16
  660.7 1.8 fusion.16
  664.8 1.8 fusion.16
  668.8 1.8 fusion.16
  672.9 1.8 fusion.16
  677.0 1.8 fusion.16
  721.0 2.2 add_bitcast_fusion
  (172 shorter events, 97.8 us)
Async XLA Ops:
  7.2 257.8 %copy-start = (f32[64,64]{1,0:T(8,128)S(1)}, f32[64,64]{1,0:T(8,128)}, u32[]{:S(2)}) copy-start(f32[64,64]{1,0:T(8,128)} %param.11) | copy-start | bytes 49156
  7.2 257.8 %reduce-scatter.2.cloned.1.call-start = ((), (), s32[]{:S(2)}) async-start(), calls=%async_computation.2 | async-start | bytes 557056 | tf_op jit(solution)/shard_map/reduce_scatter | solution.py:60
  9.5 195.4 %copy-start.4 = (bf16[1,2048,128]{2,1,0:T(8,128)(2,1)S(1)}, bf16[1,2048,128]{2,1,0:T(8,128)(2,1)}, u32[]{:S(2)}) copy-start(bf16[1,2048,128]{2,1,0:T(8,128)(2,1)} %param.8) | copy-start | bytes 1572868
  205.0 2.4 copy-start.7
  205.0 62.5 %copy-start.6 = (f32[1,2048]{1,0:T(1,128)S(1)}, f32[1,2048]{1,0:T(1,128)}, u32[]{:S(2)}) copy-start(f32[1,2048]{1,0:T(1,128)} %param.10) | copy-start | bytes 24580
  207.3 59.3 %copy-start.1 = (f32[2048,128]{1,0:T(8,128)}, f32[2048,128]{1,0:T(8,128)S(1)}, u32[]{:S(2)}) copy-start(f32[2048,128]{1,0:T(8,128)S(1)} %fusion.7) | copy-start | bytes 3145732
  208.9 134.1 %all-gather.9.cloned.1.call-start = ((), (), s32[]{:S(2)}) async-start(), calls=%async_computation.4 | async-start | bytes 1081344 | tf_op jit(solution)/shard_map/all_gather | solution.py:16
  266.6 322.6 %all-gather.7.cloned.1.call-start = ((), (), s32[]{:S(2)}) async-start(), calls=%async_computation.3 | async-start | bytes 34603008 | tf_op jit(solution)/shard_map/all_gather | solution.py:16
  589.3 130.3 %copy-start.5 = (f32[128,64]{0,1:T(8,128)S(1)}, f32[128,64]{0,1:T(8,128)}, u32[]{:S(2)}) copy-start(f32[128,64]{0,1:T(8,128)} %convolution_negate_fusion) | copy-start | bytes 98308
  589.3 131.7 %copy-start.2 = (f32[2048,128]{1,0:T(8,128)S(1)}, f32[2048,128]{1,0:T(8,128)}, u32[]{:S(2)}) copy-start(f32[2048,128]{1,0:T(8,128)} %copy-done.1) | copy-start | bytes 3145732
  589.3 131.7 %copy-start.3 = (f32[2048,128]{1,0:T(8,128)S(1)}, f32[2048,128]{1,0:T(8,128)}, u32[]{:S(2)}) copy-start(f32[2048,128]{1,0:T(8,128)} %param.12) | copy-start | bytes 3145732
Sparse Core Ops, SparseCore 0:
  209.0 55.9 reduce-scatter.1
  269.1 73.9 all-gather.8
  347.3 241.9 all-gather.6
